TPU v7x, 256 devices: a whole 4x4x8 slice. The times are simulated.
256 devices in a mesh: img: 4 (over y), seq: 64 (over z, x, core).
Axes of the slice: x: 4, y: 4, z: 8, core: 2. Of those that a mesh axis runs over, the one named last changes fastest.
Arguments:
- query_proj: bfloat16 [4, 8192, 1280], P('img', 'seq'), may hold values from -6 to 6
- key_proj: bfloat16 [4, 8192, 1280], P('img', 'seq'), may hold values from -6 to 6
- value_proj: bfloat16 [4, 8192, 1280], P('img', 'seq'), may hold values from -12 to 12
- merge_cells: int32 [4, 2048, 4], P('img', 'seq'), may hold values from 0 to 8191, as said below
- unmerge: int32 [4, 8192], P('img', 'seq'), may hold values from 0 to 2047, as said below
- grad_out: bfloat16 [4, 8192, 1280], P('img', 'seq'), may hold values from -9 to 9
- query_gain: float32 [64], replicated, may hold values from 1 to 2.5
- key_gain: float32 [64], replicated, may hold values from 1 to 2.5
Outputs:
- attended: bfloat16 [4, 8192, 1280], P('img', 'seq')
- grad_query: bfloat16 [4, 8192, 1280], P('img', 'seq')
- grad_key: bfloat16 [4, 8192, 1280], P('img', 'seq')
- grad_value: bfloat16 [4, 8192, 1280], P('img', 'seq')
- grad_query_gain: float32 [64], replicated
- grad_key_gain: float32 [64], replicated
Inputs may be any that keep to these rules, and one draw needn't show every extreme that they name: `merge_cells`: row c of an image lists, in some order, the four tokens of one 2x2 cell: columns j and j + 1 (modulo 64) of image rows 2 i and 2 i + 1, where token r * 64 + s stands at row r and column s and j has one parity within each pair of rows; every token lies in exactly one cell; cell c and its four tokens are held by the same seq index. `unmerge`: entry t is the row of merge_cells of the same image that lists token t.
All inputs are finite; a program needn't handle non-finite values.
Results may differ from a plain program's by a relative error of at most 0.012.
Values may be sent and summed in bfloat16 or wider, within the bound.
A program may use at most 128 MiB of HBM per device.

v0:
```python
import math
import jax
import jax.numpy as jnp
from jax import lax
from jax.sharding import PartitionSpec as P

EPSILON = 1e-06
PRECISE = lax.Precision.HIGHEST


def normalize(inputs, gain_row):
    row_scale = lax.rsqrt(jnp.mean(inputs * inputs, axis=-1, keepdims=True) + EPSILON)
    unit_vals = inputs * row_scale
    return (unit_vals, row_scale, unit_vals * gain_row)


def norm_back(grad_normed, unit_vals, row_scale, gain_row):
    grad_unit = grad_normed * gain_row
    mean_inner = jnp.mean(grad_unit * unit_vals, axis=-1, keepdims=True)
    return row_scale * (grad_unit - unit_vals * mean_inner)


def attention_pass(queries, upstream, keys_all, values_all):
    tok_rows, group_heads, head_dim = queries.shape
    group_lanes = group_heads * head_dim
    cell_count = keys_all.shape[0]
    block_rows = math.gcd(cell_count, 512)
    block_count = cell_count // block_rows
    key_blocks = keys_all.reshape(block_count, block_rows, group_lanes)
    value_blocks = values_all.reshape(block_count, block_rows, group_lanes)

    def scores_of(key_rows):
        return (
            jnp.einsum(
                "thd,khd->thk",
                queries,
                key_rows.reshape(-1, group_heads, head_dim),
                preferred_element_type=jnp.float32,
            )
            * 0.125
        )

    def forward_step(running, pieces):
        row_total, weighted = running
        key_rows, value_rows = pieces
        exp_scores = jnp.exp(scores_of(key_rows))
        row_total = row_total + jnp.sum(exp_scores, axis=-1)
        weighted = weighted + jnp.einsum(
            "thk,khd->thd",
            exp_scores.astype(jnp.bfloat16),
            value_rows.reshape(-1, group_heads, head_dim),
            preferred_element_type=jnp.float32,
        )
        return ((row_total, weighted), None)

    initial = (
        jnp.zeros((tok_rows, group_heads), jnp.float32),
        jnp.zeros((tok_rows, group_heads, head_dim), jnp.float32),
    )
    (row_total, weighted), unused = lax.scan(forward_step, initial, (key_blocks, value_blocks))
    attended = (weighted / row_total[:, :, None]).astype(jnp.bfloat16)
    row_inner = jnp.sum(upstream.astype(jnp.float32) * attended.astype(jnp.float32), axis=-1)

    def local_grads(key_rows, value_rows):
        attention = jnp.exp(scores_of(key_rows)) / row_total[:, :, None]
        grad_weights = jnp.einsum(
            "thd,khd->thk",
            upstream,
            value_rows.reshape(-1, group_heads, head_dim),
            preferred_element_type=jnp.float32,
        )
        grad_scores = (attention * (grad_weights - row_inner[:, :, None])).astype(jnp.bfloat16)
        return (attention.astype(jnp.bfloat16), grad_scores)

    def key_terms(key_rows, attention_bf, grad_scores):
        row_count = key_rows.shape[0]
        grad_keys = (
            jnp.einsum("thk,thd->khd", grad_scores, queries, preferred_element_type=jnp.float32)
            * 0.125
        )
        grad_values = jnp.einsum(
            "thk,thd->khd", attention_bf, upstream, preferred_element_type=jnp.float32
        )
        return jnp.concatenate(
            [
                grad_keys.reshape(row_count, group_lanes),
                grad_values.reshape(row_count, group_lanes),
            ],
            axis=1,
        )

    def query_term(key_rows, grad_scores):
        return (
            jnp.einsum(
                "thk,khd->thd",
                grad_scores,
                key_rows.reshape(-1, group_heads, head_dim),
                preferred_element_type=jnp.float32,
            )
            * 0.125
        )

    query_zero = jnp.zeros((tok_rows, group_heads, head_dim), jnp.float32)

    def backward_step(running, pieces):
        key_rows, value_rows = pieces
        attention_bf, grad_scores = local_grads(key_rows, value_rows)
        return (
            running + query_term(key_rows, grad_scores),
            key_terms(key_rows, attention_bf, grad_scores),
        )

    grad_q_group, term_blocks = lax.scan(backward_step, query_zero, (key_blocks, value_blocks))
    return (attended, grad_q_group, term_blocks.reshape(cell_count, 2 * group_lanes), None)


def local(query_proj, key_proj, value_proj, merge_cells, unmerge, grad_out, query_gain, key_gain):
    tok_dev = query_proj.shape[1]
    total_lanes = query_proj.shape[2]
    head_dim = query_gain.shape[0]
    head_count = total_lanes // head_dim
    cells_dev = merge_cells.shape[1]
    seq_index = lax.axis_index("seq")
    q_unit, q_scale, q_normed = normalize(
        query_proj[0].astype(jnp.float32).reshape(tok_dev, head_count, head_dim), query_gain
    )
    q_bf = q_normed.reshape(tok_dev, total_lanes).astype(jnp.bfloat16)
    k_unit, k_scale, k_normed = normalize(
        key_proj[0].astype(jnp.float32).reshape(tok_dev, head_count, head_dim), key_gain
    )
    tok_ids = seq_index * tok_dev + jnp.arange(tok_dev, dtype=jnp.int32)
    member = jnp.sum(
        (merge_cells[0][:, :, None] == tok_ids[None, None, :]).astype(jnp.float32), axis=1
    )
    k_merged = (
        jnp.dot(member, k_normed.reshape(tok_dev, total_lanes), precision=PRECISE) * 0.25
    ).astype(jnp.bfloat16)
    v_merged = (
        jnp.dot(member.astype(jnp.bfloat16), value_proj[0], preferred_element_type=jnp.float32)
        * 0.25
    ).astype(jnp.bfloat16)
    group_lanes = 256
    group_heads = group_lanes // head_dim
    out_parts, query_parts, key_parts, value_parts = ([], [], [], [])
    for group_index in range(total_lanes // group_lanes):
        lane_start = group_index * group_lanes
        queries = q_bf[:, lane_start : lane_start + group_lanes].reshape(
            tok_dev, group_heads, head_dim
        )
        upstream = grad_out[0][:, lane_start : lane_start + group_lanes].reshape(
            tok_dev, group_heads, head_dim
        )
        keys_all, values_all = (
            lax.all_gather(
                k_merged[:, lane_start : lane_start + group_lanes], "seq", axis=0, tiled=True
            ),
            lax.all_gather(
                v_merged[:, lane_start : lane_start + group_lanes], "seq", axis=0, tiled=True
            ),
        )
        attended, grad_q_group, term_rows, unused = attention_pass(
            queries, upstream, keys_all, values_all
        )
        reduced = lax.psum_scatter(term_rows, "seq", scatter_dimension=0, tiled=True)
        out_parts.append(attended.reshape(tok_dev, group_lanes))
        query_parts.append(grad_q_group.reshape(tok_dev, group_lanes))
        key_parts.append(reduced[:, :group_lanes])
        value_parts.append(reduced[:, group_lanes:])
    attended_all = jnp.concatenate(out_parts, axis=1)
    grad_q_normed = jnp.concatenate(query_parts, axis=1).reshape(tok_dev, head_count, head_dim)
    grad_merged_k = jnp.concatenate(key_parts, axis=1)
    grad_merged_v = jnp.concatenate(value_parts, axis=1)
    cell_ids = seq_index * cells_dev + jnp.arange(cells_dev, dtype=jnp.int32)
    unmerge_table = (unmerge[0][:, None] == cell_ids[None, :]).astype(jnp.float32)
    grad_k_normed = (jnp.dot(unmerge_table, grad_merged_k, precision=PRECISE) * 0.25).reshape(
        tok_dev, head_count, head_dim
    )
    grad_value = (jnp.dot(unmerge_table, grad_merged_v, precision=PRECISE) * 0.25).astype(
        jnp.bfloat16
    )
    gain_terms = (
        jnp.sum(grad_q_normed * q_unit, axis=(0, 1)),
        jnp.sum(grad_k_normed * k_unit, axis=(0, 1)),
    )
    grad_query_gain, grad_key_gain = lax.psum((gain_terms[0], gain_terms[1]), ("img", "seq"))
    grad_query = (
        norm_back(grad_q_normed, q_unit, q_scale, query_gain)
        .reshape(tok_dev, total_lanes)
        .astype(jnp.bfloat16)
    )
    grad_key = (
        norm_back(grad_k_normed, k_unit, k_scale, key_gain)
        .reshape(tok_dev, total_lanes)
        .astype(jnp.bfloat16)
    )
    return (
        attended_all[None],
        grad_query[None],
        grad_key[None],
        grad_value[None],
        grad_query_gain,
        grad_key_gain,
    )


def solution(mesh):
    placed = (
        P("img", "seq", None),
        P("img", "seq", None),
        P("img", "seq", None),
        P("img", "seq", None),
        P("img", "seq"),
        P("img", "seq", None),
        P(),
        P(),
    )
    return jax.shard_map(
        local,
        mesh=mesh,
        in_specs=placed,
        out_specs=(
            P("img", "seq", None),
            P("img", "seq", None),
            P("img", "seq", None),
            P("img", "seq", None),
            P(),
            P(),
        ),
        check_vma=False,
    )
```

profile of v0, /device:TPU:1, one launch (start us, length us, event | category | flops | bytes accessed | tf_op | source)
XLA Modules:
  0.0 1611.3 jit_solution(1745395088641482915)
XLA Ops:
  22.7 71.7 %all-gather.11.cloned.1.call-done = bf16[2048,256]{1,0:T(8,128)(2,1)} async-done(((bf16[32,256]{1,0:T(8,128)(2,1)}), bf16[2048,256]{1,0:T(8,128)(2,1)}) %all-gather.11.cloned.1.call-update) | async-done | bytes 1048592 | tf_op jit(solution)/shard_map/all_gather | solution.py:154
  96.7 75.1 %all-gather.13.cloned.1.call-done = bf16[2048,256]{1,0:T(8,128)(2,1)} async-done(((bf16[32,256]{1,0:T(8,128)(2,1)}), bf16[2048,256]{1,0:T(8,128)(2,1)}) %all-gather.13.cloned.1.call-update) | async-done | bytes 1048592 | tf_op jit(solution)/shard_map/all_gather | solution.py:157
  171.8 2.3 copy.165
  174.1 14.6 while.130
  190.1 2.5 broadcast.241.clone2
  192.6 28.4 %while.135 = (s32[]{:T(128)}, f32[128,4,64]{0,2,1:T(8,128)}, f32[4,512,512]{2,1,0:T(8,128)}, bf16[4,512,256]{1,2,0:T(8,128)(2,1)}, bf16[128,4,64]{0,2,1:T(8,128)...) while((s32[]{:T(128)}, f32[128,4,64]{0,2,1:T(8,128)}, ...), condition=%wide.region_20.21_spmd.clone, body=%wide.region_19.20_spmd.clone.sunk | while | flops 169836544 | bytes 14422651 | solution.py:113
  221.0 28.1 %all-gather.15.cloned.1.call-done = bf16[2048,256]{1,0:T(8,128)(2,1)} async-done(((bf16[32,256]{1,0:T(8,128)(2,1)}), bf16[2048,256]{1,0:T(8,128)(2,1)}) %all-gather.15.cloned.1.call-update) | async-done | bytes 1048592 | tf_op jit(solution)/shard_map/all_gather | solution.py:154
  251.4 74.9 %all-gather.17.cloned.1.call-done = bf16[2048,256]{1,0:T(8,128)(2,1)} async-done(((bf16[32,256]{1,0:T(8,128)(2,1)}), bf16[2048,256]{1,0:T(8,128)(2,1)}) %all-gather.17.cloned.1.call-update) | async-done | bytes 1048592 | tf_op jit(solution)/shard_map/all_gather | solution.py:157
  328.6 10.4 while.131
  338.9 64.5 %all-gather.19.cloned.1.call-done = bf16[2048,256]{1,0:T(8,128)(2,1)} async-done(((bf16[32,256]{1,0:T(8,128)(2,1)}), bf16[2048,256]{1,0:T(8,128)(2,1)}) %all-gather.19.cloned.1.call-update) | async-done | bytes 1048592 | tf_op jit(solution)/shard_map/all_gather | solution.py:154
  405.7 74.9 %all-gather.21.cloned.1.call-done = bf16[2048,256]{1,0:T(8,128)(2,1)} async-done(((bf16[32,256]{1,0:T(8,128)(2,1)}), bf16[2048,256]{1,0:T(8,128)(2,1)}) %all-gather.21.cloned.1.call-update) | async-done | bytes 1048592 | tf_op jit(solution)/shard_map/all_gather | solution.py:157
  482.9 10.4 while.132
  493.3 64.7 %all-gather.23.cloned.1.call-done = bf16[2048,256]{1,0:T(8,128)(2,1)} async-done(((bf16[32,256]{1,0:T(8,128)(2,1)}), bf16[2048,256]{1,0:T(8,128)(2,1)}) %all-gather.23.cloned.1.call-update) | async-done | bytes 1048592 | tf_op jit(solution)/shard_map/all_gather | solution.py:154
  560.2 75.0 %all-gather.25.cloned.1.call-done = bf16[2048,256]{1,0:T(8,128)(2,1)} async-done(((bf16[32,256]{1,0:T(8,128)(2,1)}), bf16[2048,256]{1,0:T(8,128)(2,1)}) %all-gather.25.cloned.1.call-update) | async-done | bytes 1048592 | tf_op jit(solution)/shard_map/all_gather | solution.py:157
  637.6 75.1 %all-gather.27.cloned.1.call-done = bf16[2048,256]{1,0:T(8,128)(2,1)} async-done(((bf16[32,256]{1,0:T(8,128)(2,1)}), bf16[2048,256]{1,0:T(8,128)(2,1)}) %all-gather.27.cloned.1.call-update) | async-done | bytes 1048592 | tf_op jit(solution)/shard_map/all_gather | solution.py:154
  714.9 12.2 while.133
  727.4 62.4 %all-gather.29.cloned.1.call-done = bf16[2048,256]{1,0:T(8,128)(2,1)} async-done(((bf16[32,256]{1,0:T(8,128)(2,1)}), bf16[2048,256]{1,0:T(8,128)(2,1)}) %all-gather.29.cloned.1.call-update) | async-done | bytes 1048592 | tf_op jit(solution)/shard_map/all_gather | solution.py:157
  792.1 7.0 while.134
  799.7 2.5 broadcast.241.clone2.1
  802.3 28.5 %while.136 = (s32[]{:T(128)}, f32[128,4,64]{0,2,1:T(8,128)}, f32[4,512,512]{2,1,0:T(8,128)}, bf16[4,512,256]{1,2,0:T(8,128)(2,1)}, bf16[128,4,64]{0,2,1:T(8,128)...) while((s32[]{:T(128)}, f32[128,4,64]{0,2,1:T(8,128)}, ...), condition=%wide.region_23.24_spmd.clone, body=%wide.region_22.23_spmd.clone.sunk | while | flops 169836544 | bytes 14422651 | solution.py:113
  832.4 2.6 broadcast.241.clone2.2
  835.0 23.3 %while.137 = (s32[]{:T(128)}, f32[128,4,64]{0,2,1:T(8,128)S(1)}, f32[4,512,512]{2,1,0:T(8,128)}, bf16[4,512,256]{1,2,0:T(8,128)(2,1)}, bf16[128,4,64]{0,2,1:T(8,...) while((s32[]{:T(128)}, f32[128,4,64]{0,2,1:T(8,128)S(1)}, ...), condition=%wide.region_26.27_spmd.clone, body=%wide.region_25.26_spmd.clone.sunk | while | flops 169836544 | bytes 14422651 | solution.py:113
  859.9 2.5 broadcast.241.clone2.3
  862.4 16.5 %while.138 = (s32[]{:T(128)}, f32[128,4,64]{0,2,1:T(8,128)S(1)}, f32[4,512,512]{2,1,0:T(8,128)}, bf16[4,512,256]{1,2,0:T(8,128)(2,1)}, bf16[128,4,64]{0,2,1:T(8,...) while((s32[]{:T(128)}, f32[128,4,64]{0,2,1:T(8,128)S(1)}, ...), condition=%wide.region_29.30_spmd.clone, body=%wide.region_28.29_spmd.clone.sunk | while | flops 169836544 | bytes 14422651 | solution.py:113
  880.4 2.5 broadcast.241.clone2.4
  883.0 16.5 %while.139 = (s32[]{:T(128)}, f32[128,4,64]{0,2,1:T(8,128)S(1)}, f32[4,512,512]{2,1,0:T(8,128)}, bf16[4,512,256]{1,2,0:T(8,128)(2,1)}, bf16[128,4,64]{0,2,1:T(8,...) while((s32[]{:T(128)}, f32[128,4,64]{0,2,1:T(8,128)S(1)}, ...), condition=%wide.region_32.33_spmd.clone, body=%wide.region_31.32_spmd.clone.sunk | while | flops 169836544 | bytes 14422651 | solution.py:113
  905.2 25.4 %reduce-scatter.6.cloned.1.call-done = f32[32,512]{1,0:T(8,128)} async-done(((f32[2048,512]{1,0:T(8,128)}), f32[32,512]{1,0:T(8,128)}) %reduce-scatter.6.cloned.1.call-update) | async-done | bytes 65552 | tf_op jit(solution)/shard_map/reduce_scatter | solution.py:164
  931.3 146.0 %reduce-scatter.8.cloned.1.call-done = f32[32,512]{1,0:T(8,128)} async-done(((f32[2048,512]{1,0:T(8,128)}), f32[32,512]{1,0:T(8,128)}) %reduce-scatter.8.cloned.1.call-update) | async-done | bytes 65552 | tf_op jit(solution)/shard_map/reduce_scatter | solution.py:164
  1078.1 146.1 %reduce-scatter.10.cloned.1.call-done = f32[32,512]{1,0:T(8,128)} async-done(((f32[2048,512]{1,0:T(8,128)}), f32[32,512]{1,0:T(8,128)}) %reduce-scatter.10.cloned.1.call-update) | async-done | bytes 65552 | tf_op jit(solution)/shard_map/reduce_scatter | solution.py:164
  1225.0 145.9 %reduce-scatter.12.cloned.1.call-done = f32[32,512]{1,0:T(8,128)} async-done(((f32[2048,512]{1,0:T(8,128)}), f32[32,512]{1,0:T(8,128)}) %reduce-scatter.12.cloned.1.call-update) | async-done | bytes 65552 | tf_op jit(solution)/shard_map/reduce_scatter | solution.py:164
  1371.7 145.9 %reduce-scatter.14.cloned.1.call-done = f32[32,512]{1,0:T(8,128)} async-done(((f32[2048,512]{1,0:T(8,128)}), f32[32,512]{1,0:T(8,128)}) %reduce-scatter.14.cloned.1.call-update) | async-done | bytes 65552 | tf_op jit(solution)/shard_map/reduce_scatter | solution.py:164
  1525.2 79.5 %all-reduce = (f32[64]{0:T(128)}, f32[64]{0:T(128)}) all-reduce(f32[64]{0:T(128)S(1)} %reduce_sum.179, f32[64]{0:T(128)S(1)} %reduce_sum.182), channel_id=1, replica_groups=mesh['img'=4,'seq'=64] {'img','seq'}, use_global_device_ids=true, to_apply=%region_42.43 | all-reduce | flops 128 | bytes 1024 | tf_op jit(solution)/shard_map/psum | solution.py:185
  (465 shorter events, 224.7 us)
Async XLA Ops:
  7.2 12.6 copy-start.22
  7.2 13.8 copy-start.38
  7.2 87.2 %all-gather.11.cloned.1.call-start = ((), (), s32[]{:S(2)}) async-start(), calls=%async_computation.5 | async-start | bytes 1064960 | tf_op jit(solution)/shard_map/all_gather | solution.py:154
  7.3 14.8 copy-start.23
  9.6 87.1 %copy-start.2 = (f32[128,1280]{1,0:T(8,128)}, f32[128,1280]{1,0:T(8,128)S(1)}, u32[]{:S(2)}) copy-start(f32[128,1280]{1,0:T(8,128)S(1)} %copy.162) | copy-start | bytes 1966084
  13.4 158.4 %all-gather.13.cloned.1.call-start = ((), (), s32[]{:S(2)}) async-start(), calls=%async_computation.6 | async-start | bytes 1064960 | tf_op jit(solution)/shard_map/all_gather | solution.py:157
  14.3 234.8 %all-gather.15.cloned.1.call-start = ((), (), s32[]{:S(2)}) async-start(), calls=%async_computation.7 | async-start | bytes 1064960 | tf_op jit(solution)/shard_map/all_gather | solution.py:154
  15.0 311.3 %all-gather.17.cloned.1.call-start = ((), (), s32[]{:S(2)}) async-start(), calls=%async_computation.8 | async-start | bytes 1064960 | tf_op jit(solution)/shard_map/all_gather | solution.py:157
  15.6 387.9 %all-gather.19.cloned.1.call-start = ((), (), s32[]{:S(2)}) async-start(), calls=%async_computation.9 | async-start | bytes 1064960 | tf_op jit(solution)/shard_map/all_gather | solution.py:154
  16.2 464.5 %all-gather.21.cloned.1.call-start = ((), (), s32[]{:S(2)}) async-start(), calls=%async_computation.10 | async-start | bytes 1064960 | tf_op jit(solution)/shard_map/all_gather | solution.py:157
  16.8 541.2 %all-gather.23.cloned.1.call-start = ((), (), s32[]{:S(2)}) async-start(), calls=%async_computation.11 | async-start | bytes 1064960 | tf_op jit(solution)/shard_map/all_gather | solution.py:154
  17.5 617.8 %all-gather.25.cloned.1.call-start = ((), (), s32[]{:S(2)}) async-start(), calls=%async_computation.12 | async-start | bytes 1064960 | tf_op jit(solution)/shard_map/all_gather | solution.py:157
  18.3 694.4 %all-gather.27.cloned.1.call-start = ((), (), s32[]{:S(2)}) async-start(), calls=%async_computation.13 | async-start | bytes 1064960 | tf_op jit(solution)/shard_map/all_gather | solution.py:154
  19.0 770.8 %all-gather.29.cloned.1.call-start = ((), (), s32[]{:S(2)}) async-start(), calls=%async_computation.14 | async-start | bytes 1064960 | tf_op jit(solution)/shard_map/all_gather | solution.py:157
  19.6 911.0 %reduce-scatter.6.cloned.1.call-start = ((), (), s32[]{:S(2)}) async-start(), calls=%async_computation.15 | async-start | bytes 4259840 | tf_op jit(solution)/shard_map/reduce_scatter | solution.py:164
  221.0 107.6 %copy-start.16 = (f32[128,4,64]{0,2,1:T(8,128)S(1)}, f32[128,4,64]{0,2,1:T(8,128)}, u32[]{:S(2)}) copy-start(f32[128,4,64]{0,2,1:T(8,128)} %custom-call.3) | copy-start | bytes 393220
  221.0 107.6 %copy-start.37 = (f32[128,4]{0,1:T(4,128)S(1)}, f32[128,4]{0,1:T(4,128)}, u32[]{:S(2)}) copy-start(f32[128,4]{0,1:T(4,128)} %custom-call.2) | copy-start | bytes 6148
  338.9 144.0 %copy-start.13 = (f32[128,4,64]{0,2,1:T(8,128)S(1)}, f32[128,4,64]{0,2,1:T(8,128)}, u32[]{:S(2)}) copy-start(f32[128,4,64]{0,2,1:T(8,128)} %custom-call.5) | copy-start | bytes 393220
  493.3 221.6 %copy-start.14 = (f32[128,4,64]{0,2,1:T(8,128)}, f32[128,4,64]{0,2,1:T(8,128)S(1)}, u32[]{:S(2)}) copy-start(f32[128,4,64]{0,2,1:T(8,128)S(1)} %get-tuple-element.415) | copy-start | bytes 393220
  493.3 221.6 %copy-start.20 = (bf16[128,256]{0,1:T(8,128)(2,1)S(1)}, bf16[128,256]{0,1:T(8,128)(2,1)}, u32[]{:S(2)}) copy-start(bf16[128,256]{0,1:T(8,128)(2,1)} %get-tuple-element.1122) | copy-start | bytes 196612
  727.1 64.9 %copy-start.10 = (f32[128,4,64]{0,2,1:T(8,128)S(1)}, f32[128,4,64]{0,2,1:T(8,128)}, u32[]{:S(2)}) copy-start(f32[128,4,64]{0,2,1:T(8,128)} %custom-call.9) | copy-start | bytes 393220
  727.2 350.1 %reduce-scatter.8.cloned.1.call-start = ((), (), s32[]{:S(2)}) async-start(), calls=%async_computation.16 | async-start | bytes 4259840 | tf_op jit(solution)/shard_map/reduce_scatter | solution.py:164
  830.8 393.4 %reduce-scatter.10.cloned.1.call-start = ((), (), s32[]{:S(2)}) async-start(), calls=%async_computation.17 | async-start | bytes 4259840 | tf_op jit(solution)/shard_map/reduce_scatter | solution.py:164
  858.3 512.7 %reduce-scatter.12.cloned.1.call-start = ((), (), s32[]{:S(2)}) async-start(), calls=%async_computation.18 | async-start | bytes 4259840 | tf_op jit(solution)/shard_map/reduce_scatter | solution.py:164
  878.9 638.7 %reduce-scatter.14.cloned.1.call-start = ((), (), s32[]{:S(2)}) async-start(), calls=%async_computation.19 | async-start | bytes 4259840 | tf_op jit(solution)/shard_map/reduce_scatter | solution.py:164
  899.7 619.4 %copy-start.41 = (s32[1,128]{1,0:T(1,128)S(1)}, s32[1,128]{1,0:T(1,128)}, u32[]{:S(2)}) copy-start(s32[1,128]{1,0:T(1,128)} %param.32) | copy-start | bytes 1540
  900.6 620.9 %copy-start.5 = (f32[1,128,1280]{1,2,0:T(8,128)S(1)}, f32[1,128,1280]{1,2,0:T(8,128)}, u32[]{:S(2)}) copy-start(f32[1,128,1280]{1,2,0:T(8,128)} %copy-done.4) | copy-start | bytes 1966084
  900.6 620.8 %copy-start.32 = (f32[128,20]{0,1:T(8,128)S(1)}, f32[128,20]{0,1:T(8,128)}, u32[]{:S(2)}) copy-start(f32[128,20]{0,1:T(8,128)} %copy-done.31) | copy-start | bytes 30724
  900.6 620.8 %copy-start.40 = (f32[64]{0:T(128)S(1)}, f32[64]{0:T(128)}, u32[]{:S(2)}) copy-start(f32[64]{0:T(128)} %param.35) | copy-start | bytes 772
  902.4 620.6 %copy-start.3 = (f32[128,1280]{1,0:T(8,128)S(1)}, f32[128,1280]{1,0:T(8,128)}, u32[]{:S(2)}) copy-start(f32[128,1280]{1,0:T(8,128)} %copy-done.2) | copy-start | bytes 1966084
  902.4 620.6 %copy-start.18 = (bf16[1,128,1280]{2,1,0:T(8,128)(2,1)S(1)}, bf16[1,128,1280]{2,1,0:T(8,128)(2,1)}, u32[]{:S(2)}) copy-start(bf16[1,128,1280]{2,1,0:T(8,128)(2,1)} %param.29) | copy-start | bytes 983044
  1519.1 85.6 %copy-start.1 = (bf16[1,128,1280]{2,1,0:T(8,128)(2,1)S(1)}, bf16[1,128,1280]{2,1,0:T(8,128)(2,1)}, u32[]{:S(2)}) copy-start(bf16[1,128,1280]{2,1,0:T(8,128)(2,1)} %param.30) | copy-start | bytes 983044
  (26 other events, 55.6 us)
Sparse Core Ops, SparseCore 0:
  13.5 80.9 all-gather.10
  97.2 74.5 all-gather.12
  174.5 74.5 all-gather.14
  251.7 74.5 all-gather.16
  328.9 74.5 all-gather.18
  406.1 74.5 all-gather.20
  483.4 74.5 all-gather.22
  560.7 74.5 all-gather.24
  638.1 74.5 all-gather.26
  715.2 74.5 all-gather.28
  793.9 136.5 reduce-scatter.5
  934.5 142.7 reduce-scatter.7
  1081.4 142.7 reduce-scatter.9
  1228.2 142.6 reduce-scatter.11
  1374.9 142.6 reduce-scatter.13
where the time goes:
time: 1620 us; the launch traced here: 1610 us
  waiting for transfers between devices  1280 us (79%)
  local copies, waits for them, and re-layouts  124 us (8%)
  matrix products  93.7 us (6%)
  blocking collectives  79.5 us (5%)
  other arithmetic  16.3 us (1%)
    reduce_scatter x5, waiting for transfers between devices, local(): lax.psum_scatter(term_rows, 'seq', scatter_dimension=0, tiled=True)  609 us
    all_gather x5, waiting for transfers between devices, local(): lax.all_gather(v_merged[:, lane_start:lane_start + group_lanes], 'seq', a...  362 us
    all_gather x5, waiting for transfers between devices, local(): lax.all_gather(k_merged[:, lane_start:lane_start + group_lanes], 'seq', a...  304 us
    psum x1, blocking collectives, local(): lax.psum((gain_terms[0], gain_terms[1]), ('img', 'seq'))  79.5 us
    dynamic_slice x40, local copies, waits for them, and re-layouts, attention_pass(): lax.scan(forward_step, initial, (key_blocks, value_blocks))  42.7 us
    dot_general x40, matrix products, scores_of(): jnp.einsum('thd,khd->thk', queries, key_rows.reshape(-1, group_heads, hea...  35.5 us
    unnamed x111, local copies, waits for them, and re-layouts  32.6 us
  transfers between devices with their start and end apart: 15, of which 15 were waited for; matrix products, arithmetic and copies ran while one was open for 14% of the time, Pallas kernels for 0%

commit v1 on v0

--- a/solution.py
+++ b/solution.py
@@ -154,8 +154,16 @@
             lax.all_gather(
                 k_merged[:, lane_start : lane_start + group_lanes], "seq", axis=0, tiled=True
             ),
-            lax.all_gather(
-                v_merged[:, lane_start : lane_start + group_lanes], "seq", axis=0, tiled=True
+            jnp.concatenate(
+                lax.all_to_all(
+                    jnp.stack(
+                        [v_merged[:, lane_start : lane_start + group_lanes]] * lax.axis_size("seq")
+                    ),
+                    "seq",
+                    0,
+                    0,
+                ),
+                axis=0,
             ),
         )
         attended, grad_q_group, term_rows, unused = attention_pass(

time: 1620 us -> 1230 us (0.76)
  waiting for transfers between devices: 1280 us -> 858 us
  starting transfers between devices: 0.77 us -> 40.4 us
    all_gather x5 -> x0, waiting for transfers between devices: 362 us -> none  [local(): lax.all_gather(v_merged[:, lane_start:lane_start + group_lanes], 'seq', a...]
    all_gather x5, waiting for transfers between devices: 304 us -> 244 us  [local(): lax.all_gather(k_merged[:, lane_start:lane_start + group_lanes], 'seq', a...]
    all_to_all x0 -> x5, starting transfers between devices: none -> 39.8 us  [local(): lax.all_to_all(jnp.stack([v_merged[:, lane_start:lane_start + group_lanes...]
    unnamed x111 -> x129, local copies, waits for them, and re-layouts: 32.6 us -> 32.6 us
  transfers between devices with their start and end apart: 15 -> 15, of which waited for: 15 -> 11; matrix products, arithmetic and copies ran while one was open for 14% -> 18% of each run, Pallas kernels for 0% -> 0%
where the time goes in v1:
time: 1230 us
  waiting for transfers between devices  858 us (70%)
  local copies, waits for them, and re-layouts  131 us (11%)
  matrix products  88.4 us (7%)
  blocking collectives  79.7 us (6%)
  starting transfers between devices  40.4 us (3%)
  other arithmetic  15.5 us (1%)
  between operations  15.1 us (1%)
    reduce_scatter x5, waiting for transfers between devices, local(): lax.psum_scatter(term_rows, 'seq', scatter_dimension=0, tiled=True)  601 us
    all_gather x5, waiting for transfers between devices, local(): lax.all_gather(k_merged[:, lane_start:lane_start + group_lanes], 'seq', a...  244 us
    psum x1, blocking collectives, local(): lax.psum((gain_terms[0], gain_terms[1]), ('img', 'seq'))  79.7 us
    dynamic_slice x40, local copies, waits for them, and re-layouts, attention_pass(): lax.scan(forward_step, initial, (key_blocks, value_blocks))  42.8 us
    all_to_all x5, starting transfers between devices, local(): lax.all_to_all(jnp.stack([v_merged[:, lane_start:lane_start + group_lanes...  39.8 us
    dot_general x40, matrix products, scores_of(): jnp.einsum('thd,khd->thk', queries, key_rows.reshape(-1, group_heads, hea...  35.5 us
    unnamed x129, local copies, waits for them, and re-layouts  32.6 us
    dynamic_update_slice x40, local copies, waits for them, and re-layouts, attention_pass(): lax.scan(backward_step, query_zero, (key_blocks, value_blocks))  28 us
  transfers between devices with their start and end apart: 15, of which 11 were waited for; matrix products, arithmetic and copies ran while one was open for 18% of the time, Pallas kernels for 0%

profile of v1, /device:TPU:1, one launch (start us, length us, event | category | flops | bytes accessed | tf_op | source)
XLA Modules:
  0.0 1229.0 jit_solution(17603475715891383630)
XLA Ops:
  17.3 13.0 %all-to-all-start = ((bf16[64,32,256]{2,1,0:T(8,128)(2,1)}), bf16[64,32,256]{2,1,0:T(8,128)(2,1)S(1)}, u32[]{:S(2)}, u32[]{:S(2)}) async-start(bf16[64,32,256]{2,1,0:T(8,128)(2,1)} %stack.10), calls=%async_computation | async-start | bytes 2097152 | tf_op jit(solution)/shard_map/all_to_all | solution.py:158
  33.9 60.7 %all-gather.6.cloned.1.call-done = bf16[2048,256]{1,0:T(8,128)(2,1)} async-done(((bf16[32,256]{1,0:T(8,128)(2,1)}), bf16[2048,256]{1,0:T(8,128)(2,1)}) %all-gather.6.cloned.1.call-update) | async-done | bytes 1048592 | tf_op jit(solution)/shard_map/all_gather | solution.py:154
  98.8 6.7 all-to-all-start.1
  105.6 2.3 copy.155
  107.9 14.7 %while.130 = (s32[]{:T(128)}, f32[128,4]{0,1:T(4,128)}, f32[128,4,64]{0,2,1:T(8,128)S(1)}, bf16[4,512,256]{1,2,0:T(8,128)(2,1)}, bf16[128,4,64]{0,2,1:T(8,128)(2...) while((s32[]{:T(128)}, f32[128,4]{0,1:T(4,128)}, f32[128,4,64]{0,2,1:T(8,128)S(1)}, ...), condition=%wide.region_5.6_spmd.clone, body=%wide.region_3.5_spmd.clone.sunk | while | flops 67961344 | bytes 2957412 | solution.py:60
  123.9 10.4 all-to-all-done.1
  135.6 6.4 all-to-all-start.2
  142.1 2.5 broadcast.251.clone2
  144.6 28.5 %while.135 = (s32[]{:T(128)}, f32[128,4,64]{0,2,1:T(8,128)}, f32[4,512,512]{2,1,0:T(8,128)}, bf16[4,512,256]{1,2,0:T(8,128)(2,1)}, bf16[128,4,64]{0,2,1:T(8,128)...) while((s32[]{:T(128)}, f32[128,4,64]{0,2,1:T(8,128)}, ...), condition=%wide.region_20.21_spmd.clone, body=%wide.region_19.20_spmd.clone.sunk | while | flops 169836544 | bytes 14422651 | solution.py:113
  178.8 73.0 %all-gather.10.cloned.1.call-done = bf16[2048,256]{1,0:T(8,128)(2,1)} async-done(((bf16[32,256]{1,0:T(8,128)(2,1)}), bf16[2048,256]{1,0:T(8,128)(2,1)}) %all-gather.10.cloned.1.call-update) | async-done | bytes 1048592 | tf_op jit(solution)/shard_map/all_gather | solution.py:154
  255.3 6.7 all-to-all-start.3
  264.3 65.3 %all-gather.12.cloned.1.call-done = bf16[2048,256]{1,0:T(8,128)(2,1)} async-done(((bf16[32,256]{1,0:T(8,128)(2,1)}), bf16[2048,256]{1,0:T(8,128)(2,1)}) %all-gather.12.cloned.1.call-update) | async-done | bytes 1048592 | tf_op jit(solution)/shard_map/all_gather | solution.py:154
  331.9 10.4 while.131
  343.6 6.9 all-to-all-start.4
  352.9 10.4 while.132
  363.4 43.7 %all-gather.14.cloned.1.call-done = bf16[2048,256]{1,0:T(8,128)(2,1)} async-done(((bf16[32,256]{1,0:T(8,128)(2,1)}), bf16[2048,256]{1,0:T(8,128)(2,1)}) %all-gather.14.cloned.1.call-update) | async-done | bytes 1048592 | tf_op jit(solution)/shard_map/all_gather | solution.py:154
  409.4 7.0 while.133
  417.8 7.0 while.134
  425.5 2.5 broadcast.251.clone2.1
  428.0 28.6 %while.136 = (s32[]{:T(128)}, f32[128,4,64]{0,2,1:T(8,128)}, f32[4,512,512]{2,1,0:T(8,128)}, bf16[4,512,256]{1,2,0:T(8,128)(2,1)}, bf16[128,4,64]{0,2,1:T(8,128)...) while((s32[]{:T(128)}, f32[128,4,64]{0,2,1:T(8,128)}, ...), condition=%wide.region_23.24_spmd.clone, body=%wide.region_22.23_spmd.clone.sunk | while | flops 169836544 | bytes 14422651 | solution.py:113
  458.1 2.6 broadcast.251.clone2.2
  460.7 23.3 %while.137 = (s32[]{:T(128)}, f32[128,4,64]{0,2,1:T(8,128)S(1)}, f32[4,512,512]{2,1,0:T(8,128)}, bf16[4,512,256]{1,2,0:T(8,128)(2,1)}, bf16[128,4,64]{0,2,1:T(8,...) while((s32[]{:T(128)}, f32[128,4,64]{0,2,1:T(8,128)S(1)}, ...), condition=%wide.region_26.27_spmd.clone, body=%wide.region_25.26_spmd.clone.sunk | while | flops 169836544 | bytes 14422651 | solution.py:113
  485.6 2.5 broadcast.251.clone2.3
  488.1 16.6 %while.138 = (s32[]{:T(128)}, f32[128,4,64]{0,2,1:T(8,128)S(1)}, f32[4,512,512]{2,1,0:T(8,128)}, bf16[4,512,256]{1,2,0:T(8,128)(2,1)}, bf16[128,4,64]{0,2,1:T(8,...) while((s32[]{:T(128)}, f32[128,4,64]{0,2,1:T(8,128)S(1)}, ...), condition=%wide.region_29.30_spmd.clone, body=%wide.region_28.29_spmd.clone.sunk | while | flops 169836544 | bytes 14422651 | solution.py:113
  506.2 2.5 broadcast.251.clone2.4
  508.7 16.6 %while.139 = (s32[]{:T(128)}, f32[128,4,64]{0,2,1:T(8,128)S(1)}, f32[4,512,512]{2,1,0:T(8,128)}, bf16[4,512,256]{1,2,0:T(8,128)(2,1)}, bf16[128,4,64]{0,2,1:T(8,...) while((s32[]{:T(128)}, f32[128,4,64]{0,2,1:T(8,128)S(1)}, ...), condition=%wide.region_32.33_spmd.clone, body=%wide.region_31.32_spmd.clone.sunk | while | flops 169836544 | bytes 14422651 | solution.py:113
  531.0 16.8 %reduce-scatter.6.cloned.1.call-done = f32[32,512]{1,0:T(8,128)} async-done(((f32[2048,512]{1,0:T(8,128)}), f32[32,512]{1,0:T(8,128)}) %reduce-scatter.6.cloned.1.call-update) | async-done | bytes 65552 | tf_op jit(solution)/shard_map/reduce_scatter | solution.py:172
  548.5 146.1 %reduce-scatter.8.cloned.1.call-done = f32[32,512]{1,0:T(8,128)} async-done(((f32[2048,512]{1,0:T(8,128)}), f32[32,512]{1,0:T(8,128)}) %reduce-scatter.8.cloned.1.call-update) | async-done | bytes 65552 | tf_op jit(solution)/shard_map/reduce_scatter | solution.py:172
  695.4 146.1 %reduce-scatter.10.cloned.1.call-done = f32[32,512]{1,0:T(8,128)} async-done(((f32[2048,512]{1,0:T(8,128)}), f32[32,512]{1,0:T(8,128)}) %reduce-scatter.10.cloned.1.call-update) | async-done | bytes 65552 | tf_op jit(solution)/shard_map/reduce_scatter | solution.py:172
  842.3 146.0 %reduce-scatter.12.cloned.1.call-done = f32[32,512]{1,0:T(8,128)} async-done(((f32[2048,512]{1,0:T(8,128)}), f32[32,512]{1,0:T(8,128)}) %reduce-scatter.12.cloned.1.call-update) | async-done | bytes 65552 | tf_op jit(solution)/shard_map/reduce_scatter | solution.py:172
  989.0 145.9 %reduce-scatter.14.cloned.1.call-done = f32[32,512]{1,0:T(8,128)} async-done(((f32[2048,512]{1,0:T(8,128)}), f32[32,512]{1,0:T(8,128)}) %reduce-scatter.14.cloned.1.call-update) | async-done | bytes 65552 | tf_op jit(solution)/shard_map/reduce_scatter | solution.py:172
  1142.5 79.7 %all-reduce = (f32[64]{0:T(128)}, f32[64]{0:T(128)}) all-reduce(f32[64]{0:T(128)S(1)} %reduce_sum.179, f32[64]{0:T(128)S(1)} %reduce_sum.182), channel_id=1, replica_groups=mesh['img'=4,'seq'=64] {'img','seq'}, use_global_device_ids=true, to_apply=%region_42.43 | all-reduce | flops 128 | bytes 1024 | tf_op jit(solution)/shard_map/psum | solution.py:193
  (483 shorter events, 223.8 us)
Async XLA Ops:
  7.2 87.5 %all-gather.6.cloned.1.call-start = ((), (), s32[]{:S(2)}) async-start(), calls=%async_computation.10 | async-start | bytes 1064960 | tf_op jit(solution)/shard_map/all_gather | solution.py:154
  9.5 23.7 %copy-start.2 = (f32[128,1280]{1,0:T(8,128)}, f32[128,1280]{1,0:T(8,128)S(1)}, u32[]{:S(2)}) copy-start(f32[128,1280]{1,0:T(8,128)S(1)} %copy.152) | copy-start | bytes 1966084
  13.3 161.0 %all-gather.8.cloned.1.call-start = ((), (), s32[]{:S(2)}) async-start(), calls=%async_computation.11 | async-start | bytes 1064960 | tf_op jit(solution)/shard_map/all_gather | solution.py:154
  14.0 237.8 %all-gather.10.cloned.1.call-start = ((), (), s32[]{:S(2)}) async-start(), calls=%async_computation.12 | async-start | bytes 1064960 | tf_op jit(solution)/shard_map/all_gather | solution.py:154
  14.8 314.8 %all-gather.12.cloned.1.call-start = ((), (), s32[]{:S(2)}) async-start(), calls=%async_computation.13 | async-start | bytes 1064960 | tf_op jit(solution)/shard_map/all_gather | solution.py:154
  17.3 79.6 %all-to-all-start = ((bf16[64,32,256]{2,1,0:T(8,128)(2,1)}), bf16[64,32,256]{2,1,0:T(8,128)(2,1)S(1)}, u32[]{:S(2)}, u32[]{:S(2)}) async-start(bf16[64,32,256]{2,1,0:T(8,128)(2,1)} %stack.10), calls=%async_computation | async-start | bytes 2097152 | tf_op jit(solution)/shard_map/all_to_all | solution.py:158
  30.3 376.8 %all-gather.14.cloned.1.call-start = ((), (), s32[]{:S(2)}) async-start(), calls=%async_computation.14 | async-start | bytes 1064960 | tf_op jit(solution)/shard_map/all_gather | solution.py:154
  31.2 67.6 %copy-start.6 = (bf16[1,128,1280]{1,2,0:T(8,128)(2,1)}, bf16[1,128,1280]{1,2,0:T(8,128)(2,1)S(1)}, u32[]{:S(2)}) copy-start(bf16[1,128,1280]{1,2,0:T(8,128)(2,1)S(1)} %copy.153) | copy-start | bytes 983044
  33.0 74.9 %copy-start.35 = (f32[128,20]{0,1:T(8,128)}, f32[128,20]{0,1:T(8,128)S(1)}, u32[]{:S(2)}) copy-start(f32[128,20]{0,1:T(8,128)S(1)} %add_rsqrt_fusion) | copy-start | bytes 30724
  98.8 35.5 %all-to-all-start.1 = ((bf16[64,32,256]{2,1,0:T(8,128)(2,1)}), bf16[64,32,256]{2,1,0:T(8,128)(2,1)S(1)}, u32[]{:S(2)}, u32[]{:S(2)}) async-start(bf16[64,32,256]{2,1,0:T(8,128)(2,1)} %stack.11), calls=%async_computation.1 | async-start | bytes 2097152 | tf_op jit(solution)/shard_map/all_to_all | solution.py:158
  107.9 26.5 %copy-start.46 = (bf16[32,256]{1,0:T(8,128)(2,1)S(1)}, bf16[32,256]{1,0:T(8,128)(2,1)}, u32[]{:S(2)}) copy-start(bf16[32,256]{1,0:T(8,128)(2,1)} %get-tuple-element.1133) | copy-start | bytes 49156
  135.6 118.5 %all-to-all-start.2 = ((bf16[64,32,256]{2,1,0:T(8,128)(2,1)}), bf16[64,32,256]{2,1,0:T(8,128)(2,1)}, u32[]{:S(2)}, u32[]{:S(2)}) async-start(bf16[64,32,256]{2,1,0:T(8,128)(2,1)} %stack.12), calls=%async_computation.2 | async-start | bytes 2097152 | tf_op jit(solution)/shard_map/all_to_all | solution.py:158
  173.1 81.0 %copy-start.45 = (bf16[32,256]{1,0:T(8,128)(2,1)S(1)}, bf16[32,256]{1,0:T(8,128)(2,1)}, u32[]{:S(2)}) copy-start(bf16[32,256]{1,0:T(8,128)(2,1)} %get-tuple-element.1132) | copy-start | bytes 49156
  254.1 77.7 %copy-start.19 = (f32[128,4,64]{0,2,1:T(8,128)S(1)}, f32[128,4,64]{0,2,1:T(8,128)}, u32[]{:S(2)}) copy-start(f32[128,4,64]{0,2,1:T(8,128)} %custom-call.3) | copy-start | bytes 393220
  254.1 77.7 %copy-start.43 = (f32[128,4]{0,1:T(4,128)S(1)}, f32[128,4]{0,1:T(4,128)}, u32[]{:S(2)}) copy-start(f32[128,4]{0,1:T(4,128)} %custom-call.2) | copy-start | bytes 6148
  255.3 87.0 %all-to-all-start.3 = ((bf16[64,32,256]{2,1,0:T(8,128)(2,1)}), bf16[64,32,256]{2,1,0:T(8,128)(2,1)S(1)}, u32[]{:S(2)}, u32[]{:S(2)}) async-start(bf16[64,32,256]{2,1,0:T(8,128)(2,1)} %stack.13), calls=%async_computation.3 | async-start | bytes 2097152 | tf_op jit(solution)/shard_map/all_to_all | solution.py:158
  343.6 72.8 %all-to-all-start.4 = ((bf16[64,32,256]{2,1,0:T(8,128)(2,1)}), bf16[64,32,256]{2,1,0:T(8,128)(2,1)S(1)}, u32[]{:S(2)}, u32[]{:S(2)}) async-start(bf16[64,32,256]{2,1,0:T(8,128)(2,1)} %stack.14), calls=%async_computation.4 | async-start | bytes 2097152 | tf_op jit(solution)/shard_map/all_to_all | solution.py:158
  350.5 197.2 %reduce-scatter.6.cloned.1.call-start = ((), (), s32[]{:S(2)}) async-start(), calls=%async_computation.15 | async-start | bytes 4259840 | tf_op jit(solution)/shard_map/reduce_scatter | solution.py:172
  363.3 46.1 %copy-start.17 = (f32[128,4,64]{0,2,1:T(8,128)}, f32[128,4,64]{0,2,1:T(8,128)S(1)}, u32[]{:S(2)}) copy-start(f32[128,4,64]{0,2,1:T(8,128)S(1)} %get-tuple-element.415) | copy-start | bytes 393220
  363.3 46.1 %copy-start.13 = (f32[128,4,64]{0,2,1:T(8,128)S(1)}, f32[128,4,64]{0,2,1:T(8,128)}, u32[]{:S(2)}) copy-start(f32[128,4,64]{0,2,1:T(8,128)} %custom-call.7) | copy-start | bytes 393220
  363.3 46.1 %copy-start.26 = (bf16[128,256]{0,1:T(8,128)(2,1)S(1)}, bf16[128,256]{0,1:T(8,128)(2,1)}, u32[]{:S(2)}) copy-start(bf16[128,256]{0,1:T(8,128)(2,1)} %get-tuple-element.1122) | copy-start | bytes 196612
  363.3 331.3 %reduce-scatter.8.cloned.1.call-start = ((), (), s32[]{:S(2)}) async-start(), calls=%async_computation.16 | async-start | bytes 4259840 | tf_op jit(solution)/shard_map/reduce_scatter | solution.py:172
  456.6 384.9 %reduce-scatter.10.cloned.1.call-start = ((), (), s32[]{:S(2)}) async-start(), calls=%async_computation.17 | async-start | bytes 4259840 | tf_op jit(solution)/shard_map/reduce_scatter | solution.py:172
  484.1 504.2 %reduce-scatter.12.cloned.1.call-start = ((), (), s32[]{:S(2)}) async-start(), calls=%async_computation.18 | async-start | bytes 4259840 | tf_op jit(solution)/shard_map/reduce_scatter | solution.py:172
  504.6 630.3 %reduce-scatter.14.cloned.1.call-start = ((), (), s32[]{:S(2)}) async-start(), calls=%async_computation.19 | async-start | bytes 4259840 | tf_op jit(solution)/shard_map/reduce_scatter | solution.py:172
  525.4 610.9 %copy-start.50 = (s32[1,128]{1,0:T(1,128)S(1)}, s32[1,128]{1,0:T(1,128)}, u32[]{:S(2)}) copy-start(s32[1,128]{1,0:T(1,128)} %param.32) | copy-start | bytes 1540
  526.3 612.3 %copy-start.5 = (f32[1,128,1280]{1,2,0:T(8,128)S(1)}, f32[1,128,1280]{1,2,0:T(8,128)}, u32[]{:S(2)}) copy-start(f32[1,128,1280]{1,2,0:T(8,128)} %copy-done.4) | copy-start | bytes 1966084
  526.3 612.3 %copy-start.38 = (f32[128,20]{0,1:T(8,128)S(1)}, f32[128,20]{0,1:T(8,128)}, u32[]{:S(2)}) copy-start(f32[128,20]{0,1:T(8,128)} %copy-done.37) | copy-start | bytes 30724
  526.3 612.3 %copy-start.49 = (f32[64]{0:T(128)S(1)}, f32[64]{0:T(128)}, u32[]{:S(2)}) copy-start(f32[64]{0:T(128)} %param.35) | copy-start | bytes 772
  528.2 612.0 %copy-start.3 = (f32[128,1280]{1,0:T(8,128)S(1)}, f32[128,1280]{1,0:T(8,128)}, u32[]{:S(2)}) copy-start(f32[128,1280]{1,0:T(8,128)} %copy-done.2) | copy-start | bytes 1966084
  528.2 612.1 %copy-start.24 = (bf16[1,128,1280]{2,1,0:T(8,128)(2,1)S(1)}, bf16[1,128,1280]{2,1,0:T(8,128)(2,1)}, u32[]{:S(2)}) copy-start(bf16[1,128,1280]{2,1,0:T(8,128)(2,1)} %param.29) | copy-start | bytes 983044
  1136.4 85.8 %copy-start.1 = (bf16[1,128,1280]{2,1,0:T(8,128)(2,1)S(1)}, bf16[1,128,1280]{2,1,0:T(8,128)(2,1)}, u32[]{:S(2)}) copy-start(bf16[1,128,1280]{2,1,0:T(8,128)(2,1)} %param.30) | copy-start | bytes 983044
  (35 other events, 177.4 us)
Sparse Core Ops, SparseCore 0:
  13.4 81.2 all-gather.5
  97.4 76.7 all-gather.7
  177.0 74.7 all-gather.9
  254.4 75.0 all-gather.11
  332.2 74.8 all-gather.13
  411.0 136.6 reduce-scatter.5
  551.9 142.6 reduce-scatter.7
  698.7 142.6 reduce-scatter.9
  845.6 142.5 reduce-scatter.11
  992.2 142.6 reduce-scatter.13
